TPU v7x, 32 devices: a whole 2x2x4 slice. The times are simulated.
32 devices in a mesh: grp: 2 (over x), px: 4 (over y, core), py: 4 (over z).
Axes of the slice: x: 2, y: 2, z: 4, core: 2. Of those that a mesh axis runs over, the one named last changes fastest.
Arguments:
- multiplier: float32 [3, 32, 16, 256, 256], P(None, 'py', None, ('grp', 'px')), may hold values from -6 to 6
- auxiliary: float32 [3, 32, 16, 256, 256], P(None, 'py', None, ('grp', 'px')), may hold values from -6 to 6
- density_start: float32 [16, 256, 256], P(None, ('grp', 'px')), may hold values from 0.5 to 2
- density_end: float32 [16, 256, 256], P(None, ('grp', 'px')), may hold values from 0.5 to 2
Outputs:
- multiplier_next: float32 [3, 32, 16, 256, 256], P(None, 'py', None, ('grp', 'px'))
- auxiliary_next: float32 [3, 32, 16, 256, 256], P(None, 'py', None, ('grp', 'px'))
All inputs are finite; a program needn't handle non-finite values.
Results may differ from a plain program's by a relative error of at most 0.0003.
Values sent between devices are 32-bit elements; how exact they have to be, the bound alone decides.
A program may use at most 128 MiB of HBM per device.

v0:
```python
import math
import jax
import jax.numpy as jnp
from jax import lax
from jax.sharding import PartitionSpec as P

NEWTON = 4
PENALTY = 1.0
PRECISE = lax.Precision.HIGHEST


def passed_along(value, axis, steps):
    count = lax.axis_size(axis)
    initial, last = (max(0, -steps), min(count, count - steps))
    return lax.ppermute(value, axis, [(source, source + steps) for source in range(initial, last)])


def from_behind(block, axis, distance):
    devices = range(lax.axis_size(axis))
    route = [((i - distance) % len(devices), i) for i in devices]
    return lax.ppermute(block, axis, route)


def cosine_table(levels):
    mode_index = lax.broadcasted_iota(jnp.int32, (levels, levels), 0)
    time_index = lax.broadcasted_iota(jnp.int32, (levels, levels), 1)
    phase_index = mode_index * (2 * time_index + 1) % (4 * levels)
    angles = phase_index.astype(jnp.float32) * (math.pi / (2 * levels))
    weights = jnp.where(mode_index == 0, math.sqrt(1.0 / levels), math.sqrt(2.0 / levels))
    return weights * jnp.cos(angles)


def difference_table(cosine):
    levels = cosine.shape[0]
    later = jnp.concatenate([cosine[:, 1:], jnp.zeros_like(cosine[:, :1])], axis=1)
    time_index = lax.broadcasted_iota(jnp.int32, (levels, levels), 1)
    return jnp.where(time_index < levels - 1, later - cosine, 0.0)


def hartley_table(length):
    row_index = lax.broadcasted_iota(jnp.int32, (length, length), 0)
    col_index = lax.broadcasted_iota(jnp.int32, (length, length), 1)
    phase_index = row_index * col_index % length
    angles = phase_index.astype(jnp.float32) * (2.0 * math.pi / length)
    return (jnp.cos(angles) + jnp.sin(angles)) / math.sqrt(length)


def spatial(field, hartley_rows, hartley_cols):
    field = jnp.einsum("ctbxy,kx->ctbky", field, hartley_rows, precision=PRECISE)
    return jnp.einsum("ctbxy,ky->ctbxk", field, hartley_cols, precision=PRECISE)


def eigenvalues(levels, row_start, row_total, row_count, col_count):
    time_modes = lax.broadcasted_iota(jnp.int32, (levels, 1, 1, 1), 0).astype(jnp.float32)
    row_modes = (row_start + lax.broadcasted_iota(jnp.int32, (1, 1, row_total, 1), 2)).astype(
        jnp.float32
    )
    col_modes = lax.broadcasted_iota(jnp.int32, (1, 1, 1, col_count), 3).astype(jnp.float32)
    time_part = 4.0 * jnp.sin(time_modes * (math.pi / (2 * levels))) ** 2
    row_part = 4.0 * jnp.sin(row_modes * (math.pi / row_count)) ** 2
    col_part = 4.0 * jnp.sin(col_modes * (math.pi / col_count)) ** 2
    return time_part + row_part + col_part


def project(target):
    time_part = target[0]
    space_first = target[1]
    space_second = target[2]
    kinetic = 0.5 * (space_first * space_first + space_second * space_second)
    offset_one = 1.0 + time_part
    scaling = jnp.maximum(offset_one, 1.0) + jnp.cbrt(kinetic)
    for newton_step in range(NEWTON):
        residue = scaling * scaling * (scaling - offset_one) - kinetic
        derivative = scaling * (3.0 * scaling - 2.0 * offset_one)
        scaling = jnp.maximum(scaling - residue / derivative, 1.0)
    feasible = time_part + kinetic <= 0.0
    return jnp.stack(
        [
            jnp.where(feasible, time_part, time_part - (scaling - 1.0)),
            jnp.where(feasible, space_first, space_first / scaling),
            jnp.where(feasible, space_second, space_second / scaling),
        ]
    )


def local(multiplier, auxiliary, density_start, density_end):
    levels_here = multiplier.shape[1]
    levels = levels_here * lax.axis_size("py")
    first_level = lax.axis_index("py") * levels_here
    level_index = first_level + lax.broadcasted_iota(jnp.int32, (levels_here, 1, 1, 1), 0)
    offset_field = auxiliary - multiplier / PENALTY
    offset_time = jnp.where(level_index == levels - 1, 0.0, offset_field[0])
    boundary = jnp.where(level_index == 0, -density_start / PENALTY, 0.0) + jnp.where(
        level_index == levels - 1, density_end / PENALTY, 0.0
    )
    offset_second = offset_field[2]
    source = jnp.roll(offset_second, 1, axis=3) - offset_second + boundary
    before = passed_along(offset_time[levels_here - 1 :], "py", 1)
    earlier = jnp.concatenate([before, offset_time[: levels_here - 1]], axis=0)
    offset_along = offset_field[1]
    rows_here = offset_along.shape[2]
    left_rim = from_behind(offset_along[:, :, rows_here - 1 :, :], ("grp", "px"), 1)
    beside = jnp.concatenate([left_rim, offset_along[:, :, : rows_here - 1, :]], axis=2)
    payload = (earlier - offset_time + beside - offset_along + source)[None]
    pencil = lax.all_to_all(payload, ("grp", "px"), split_axis=2, concat_axis=3, tiled=True)
    row_count = pencil.shape[3]
    col_count = pencil.shape[4]
    hartley_rows = hartley_table(row_count)
    hartley_cols = hartley_table(col_count)
    spectral = spatial(pencil, hartley_rows, hartley_cols)
    mode_data = lax.all_to_all(spectral, "py", split_axis=3, concat_axis=1, tiled=True)
    cosine = cosine_table(levels)
    difference = difference_table(cosine)
    rhs_modes = jnp.einsum("kt,tbxy->kbxy", cosine, mode_data[0], precision=PRECISE)
    rows_mode = mode_data.shape[3]
    eigen = eigenvalues(levels, lax.axis_index("py") * rows_mode, rows_mode, row_count, col_count)
    positive = eigen > 0.0
    inverse = jnp.where(positive, 1.0 / jnp.where(positive, eigen, 1.0), 0.0)
    potential_modes = rhs_modes * inverse
    potential = jnp.einsum("kt,kbxy->tbxy", cosine, potential_modes, precision=PRECISE)
    time_rate = jnp.einsum("kt,kbxy->tbxy", difference, potential_modes, precision=PRECISE)
    returned = lax.all_to_all(
        jnp.stack([potential, time_rate]), "py", split_axis=1, concat_axis=3, tiled=True
    )
    space_values = spatial(returned, hartley_rows, hartley_cols)
    plane_potential = space_values[0]
    gradient = jnp.stack(
        [
            space_values[1],
            jnp.roll(plane_potential, -1, axis=2) - plane_potential,
            jnp.roll(plane_potential, -1, axis=3) - plane_potential,
        ]
    )
    slab_gradient = lax.all_to_all(gradient, ("grp", "px"), split_axis=3, concat_axis=2, tiled=True)
    target = slab_gradient + multiplier / PENALTY
    auxiliary_next = project(target)
    multiplier_next = multiplier + PENALTY * (slab_gradient - auxiliary_next)
    return (multiplier_next, auxiliary_next)


def solution(mesh):
    placed = (
        P(None, "py", None, ("grp", "px"), None),
        P(None, "py", None, ("grp", "px"), None),
        P(None, ("grp", "px"), None),
        P(None, ("grp", "px"), None),
    )
    return jax.shard_map(
        local,
        mesh=mesh,
        in_specs=placed,
        out_specs=(
            P(None, "py", None, ("grp", "px"), None),
            P(None, "py", None, ("grp", "px"), None),
        ),
        check_vma=False,
    )
```

profile of v0, /device:TPU:0, one launch (start us, length us, event | category | flops | bytes accessed | tf_op | source)
XLA Modules:
  0.0 775.5 jit_solution(9766000139064356499)
XLA Ops:
  0.6 22.9 %copy_subtract_fusion = f32[3,8,16,32,256]{4,2,1,3,0:T(8,128)S(1)} fusion(f32[3,8,16,32,256]{4,3,2,1,0:T(8,128)} %param.5, f32[3,8,16,32,256]{4,3,2,1,0:T(8,128)} %param.4), kind=kLoop, calls=%fused_computation.3 | loop fusion | flops 3145728 | bytes 37748736 | tf_op jit(solution)/shard_map/sub | solution.py:91
  25.7 5.8 collective-permute-start
  31.6 3.4 slice_bitcast_fusion.4
  36.1 2.6 slice_bitcast_fusion.2
  49.0 10.4 %fusion.4 = f32[1,8,16,32,256]{4,2,1,3,0:T(8,128)S(1)} fusion(f32[1,7,16,32,256]{4,2,1,3,0:T(8,128)} %slice_bitcast_fusion.7, f32[1,1,16,32,256]{4,2,1,3,0:T(8,128)} %bitcast.9, f32[1,8,16,31,256]{4,2,1,3,0:T(8,128)} %slice_bitcast_fusion.3, f32[1,8,16,1,256]{4,2,1,3,0:T(8,128)S(1)} %bitcast.104, f32[1,8,16,32,255]{4,2,1,3,0:T(8,128)} %slice_bitcast_fusion.2, ...), kind=kLoop, calls=%fused_computation.18 | loop fusion | flops 13631488 | bytes 30408720 | tf_op jit(solution)/shard_map/add | solution.py:104
  61.8 52.6 %all_to_all.66 = f32[1,8,16,32,256]{4,1,3,0,2:T(8,128)S(1)} all-to-all(f32[1,8,16,32,256]{4,1,3,0,2:T(8,128)S(1)} %copy.75), channel_id=1, replica_groups=mesh['grp'=2,'px'=4,'py'=4] {'grp','px'}, dimensions={2} | all-to-all | bytes 8388608 | tf_op jit(solution)/shard_map/all_to_all | solution.py:105
  115.7 4.8 fusion.42
  120.6 4.6 fusion.31
  125.2 5.4 copy.77
  130.6 4.9 all-to-all-start.1
  136.3 92.5 %all-to-all-done.1 = f32[1,8,2,256,256]{4,2,1,0,3:T(2,128)} async-done(((f32[1,8,2,256,256]{4,2,1,0,3:T(2,128)}), f32[1,8,2,256,256]{4,2,1,0,3:T(2,128)}, u32[]{:S(2)}, u32[]{:S(2)}) %all-to-all-start.1) | async-done | bytes 4194336 | tf_op jit(solution)/shard_map/all_to_all | solution.py:111
  228.8 6.0 fusion.6
  234.8 4.1 fusion.25
  238.9 4.1 fusion.28
  244.7 5.3 copy.80
  249.9 185.3 %all_to_all.67 = f32[2,32,2,64,256]{4,3,2,0,1:T(8,128)S(1)} all-to-all(f32[2,32,2,64,256]{4,3,2,0,1:T(8,128)S(1)} %copy.80), channel_id=1, replica_groups=mesh['grp'=2,'px'=4,'py'=4] {'py'}, dimensions={1} | all-to-all | bytes 16777216 | tf_op jit(solution)/shard_map/all_to_all | solution.py:122
  436.4 9.7 %fusion.45 = f32[256,2,8,2,256]{4,0,3,2,1:T(8,128)S(1)} fusion(f32[2,8,2,256,256]{4,3,2,1,0:T(8,128)S(1)} %bitcast.100), kind=kOutput, calls=%fused_computation.74 | convolution fusion | flops 6443499520 | bytes 16777216 | tf_op jit(solution)/shard_map/ctbxy,kx->ctbky/dot_general | solution.py:49
  446.1 8.2 %fusion = f32[2,8,2,256,256]{4,3,2,1,0:T(8,128)S(1)} fusion(f32[256,2,8,2,256]{4,0,3,2,1:T(8,128)S(1)} %fusion.45), kind=kOutput, calls=%fused_computation.7 | convolution fusion | flops 6443499520 | bytes 16777216 | tf_op jit(solution)/shard_map/ctbxy,ky->ctbxk/dot_general | solution.py:50
  454.5 3.1 copy-done.1
  457.8 3.1 slice_bitcast_fusion
  464.7 9.9 %fusion.104 = (f32[1,8,2,256,256]{4,3,2,1,0:T(8,128)S(1)}, f32[1,8,2,256,256]{4,3,2,1,0:T(8,128)}, f32[1,8,2,256,256]{4,3,2,1,0:T(8,128)}) fusion(f32[2,8,2,256,256]{4,3,2,1,0:T(8,128)} %copy-done.1, f32[1,8,2,1,256]{4,3,2,1,0:T(1,128)S(1)} %slice_bitcast_fusion.8, f32[1,8,2,255,256]{4,3,2,1,0:T(8,128)} %slice_bitcast_fusion.1, ...), kind=kLoop, calls=%fused_computation.143 | loop fusion | flops 4194304 | bytes 29360128 | tf_op jit(solution)/shard_map/slice | solution.py:129
  474.6 9.7 %pad_maximum_fusion = f32[3,8,2,256,256]{4,3,2,1,0:T(8,128)} fusion(f32[1,8,2,256,256]{4,3,2,1,0:T(8,128)} %get-tuple-element.21, f32[1,8,2,256,256]{4,3,2,1,0:T(8,128)} %get-tuple-element.20, f32[1,8,2,256,256]{4,3,2,1,0:T(8,128)S(1)} %get-tuple-element.19), kind=kLoop, calls=%fused_computation | loop fusion | flops 6291456 | bytes 25165824 | tf_op jit(solution)/shard_map/stack | solution.py:127
  484.3 21.0 %copy.85 = f32[3,8,2,256,256]{4,2,1,0,3:T(2,128)S(1)} copy(f32[3,8,2,256,256]{4,3,2,1,0:T(8,128)} %pad_maximum_fusion) | data formatting | bytes 25165824 | tf_op jit(solution)/shard_map/stack | solution.py:127
  505.3 143.1 %all_to_all.68 = f32[3,8,2,256,256]{4,2,1,0,3:T(2,128)S(1)} all-to-all(f32[3,8,2,256,256]{4,2,1,0,3:T(2,128)S(1)} %copy.85), channel_id=1, replica_groups=mesh['grp'=2,'px'=4,'py'=4] {'grp','px'}, dimensions={3} | all-to-all | bytes 25165824 | tf_op jit(solution)/shard_map/all_to_all | solution.py:134
  648.4 8.0 %copy.107 = f32[3,8,2,8,32,256]{5,2,3,1,4,0:T(2,128)} copy(f32[3,8,2,8,32,256]{5,2,1,0,4,3:T(2,128)S(1)} %bitcast.97) | data formatting | bytes 25165824 | tf_op jit(solution)/shard_map/all_to_all | solution.py:134
  656.4 15.7 %all_to_all.61 = f32[3,8,16,32,256]{4,2,1,3,0:T(8,128)} reshape(f32[3,8,8,2,32,256]{5,3,2,1,4,0:T(2,128)} %bitcast.98) | data formatting | bytes 25165824 | tf_op jit(solution)/shard_map/all_to_all | solution.py:134
  672.1 18.4 %copy_add_fusion = f32[3,8,16,32,256]{4,2,1,3,0:T(8,128)} fusion(f32[3,8,16,32,256]{4,2,1,3,0:T(8,128)} %all_to_all.61, f32[3,8,16,32,256]{4,3,2,1,0:T(8,128)} %param.4), kind=kLoop, calls=%fused_computation.5 | loop fusion | flops 3145728 | bytes 37748736 | tf_op jit(solution)/shard_map/add | solution.py:135
  690.5 14.7 %subtract_select_fusion = (f32[1,8,16,32,256]{4,2,1,3,0:T(8,128)}, f32[1,8,16,32,256]{4,2,1,3,0:T(8,128)S(1)}, pred[1,8,16,32,256]{4,2,1,3,0:T(8,128)(4,1)S(1)}) fusion(f32[3,8,16,32,256]{4,2,1,3,0:T(8,128)} %copy_add_fusion), kind=kLoop, calls=%fused_computation.11 | loop fusion | flops 55574528 | bytes 22020096 | tf_op jit(solution)/shard_map/jit(_where)/select_n | solution.py:79
  705.3 7.5 divide_select_fusion.1
  714.1 20.6 %pad_maximum_fusion.1 = (f32[3,8,16,32,256]{4,2,1,3,0:T(8,128)}, f32[3,8,16,32,256]{4,2,1,3,0:T(8,128)}) fusion(f32[1,8,16,32,256]{4,2,1,3,0:T(8,128)} %get-tuple-element.14, f32[1,8,16,32,256]{4,2,1,3,0:T(8,128)} %get-tuple-element.13, f32[1,8,16,32,256]{4,2,1,3,0:T(8,128)} %get-tuple-element.10, f32[3,8,16,32,256]{4,2,1,3,0:T(8,128)S(1)} %bitcast.96, ...), kind=kLoop, calls=%fused_computation.1 | loop fusion | flops 12582912 | bytes 62914560 | tf_op jit(solution)/shard_map/stack | solution.py:77
  734.8 20.2 %copy.90 = f32[3,8,16,32,256]{4,3,2,1,0:T(8,128)} copy(f32[3,8,16,32,256]{4,2,1,3,0:T(8,128)} %get-tuple-element.15) | data formatting | bytes 25165824
  754.9 20.4 %copy.89 = f32[3,8,16,32,256]{4,3,2,1,0:T(8,128)} copy(f32[3,8,16,32,256]{4,2,1,3,0:T(8,128)} %get-tuple-element.16) | data formatting | bytes 25165824
  (59 shorter events, 26.4 us)
Async XLA Ops:
  23.6 11.3 %copy-start = (f32[3,8,16,32,256]{4,2,1,3,0:T(8,128)}, f32[3,8,16,32,256]{4,2,1,3,0:T(8,128)S(1)}, u32[]{:S(2)}) copy-start(f32[3,8,16,32,256]{4,2,1,3,0:T(8,128)S(1)} %copy_subtract_fusion) | copy-start | bytes 37748740
  25.7 23.2 %collective-permute-start = (f32[1,16,32,256]{3,1,0,2:T(8,128)}, f32[1,16,32,256]{3,1,0,2:T(8,128)}, u32[]{:S(2)}, u32[]{:S(2)}) collective-permute-start(f32[1,16,32,256]{3,1,0,2:T(8,128)} %slice.83), channel_id=1, source_target_pairs={{0,1},{1,2},{2,3},{4,5},{5,6},{6,7},{8,9},{9,10},{10,11},{12,13},{... | collective-permute-start | bytes 1572872 | tf_op jit(solution)/shard_map/ppermute | solution.py:15
  35.8 13.1 %collective-permute-start.1 = (f32[8,16,1,256]{3,1,0,2:T(8,128)S(1)}, f32[8,16,1,256]{3,1,0,2:T(8,128)S(1)}, u32[]{:S(2)}, u32[]{:S(2)}) collective-permute-start(f32[8,16,1,256]{3,1,0,2:T(8,128)S(1)} %slice.86), channel_id=1, source_target_pairs={{28,0},{0,4},{4,8},{8,12},{12,16},{16,20},{20,24},{24,28},{29,1},{... | collective-permute-start | bytes 393224 | tf_op jit(solution)/shard_map/ppermute | solution.py:21
  36.1 3.7 copy-start.2
  42.3 2.8 copy-start.3
  44.5 1.0 copy-start.4
  130.6 98.2 %all-to-all-start.1 = ((f32[1,8,2,256,256]{4,2,1,0,3:T(2,128)}), f32[1,8,2,256,256]{4,2,1,0,3:T(2,128)}, u32[]{:S(2)}, u32[]{:S(2)}) async-start(f32[1,8,2,256,256]{4,2,1,0,3:T(2,128)} %copy.77), calls=%async_computation.1 | async-start | bytes 8388608 | tf_op jit(solution)/shard_map/all_to_all | solution.py:111
  454.2 3.4 copy-start.1
  690.5 22.3 %slice-start = ((s8[12582912]{0:T(1024)(128)(4,1)}), s8[4194304]{0:T(1024)(128)(4,1)S(1)}, s32[]{:S(2)}) async-start(s8[12582912]{0:T(1024)(128)(4,1)} %bitcast.93), calls=%async_computation.4 | async-start | bytes 8388608
  690.5 22.3 %slice-start.1 = ((s8[12582912]{0:T(1024)(128)(4,1)}), s8[4194304]{0:T(1024)(128)(4,1)S(1)}, s32[]{:S(2)}) async-start(s8[12582912]{0:T(1024)(128)(4,1)} %bitcast.93), calls=%async_computation.5 | async-start | bytes 8388608
  690.5 22.3 %slice-start.3 = ((s8[12582912]{0:T(1024)(128)(4,1)}), s8[4194304]{0:T(1024)(128)(4,1)S(1)}, s32[]{:S(2)}) async-start(s8[12582912]{0:T(1024)(128)(4,1)} %bitcast.95), calls=%async_computation.7 | async-start | bytes 8388608
  690.5 22.3 %slice-start.4 = ((s8[12582912]{0:T(1024)(128)(4,1)}), s8[4194304]{0:T(1024)(128)(4,1)S(1)}, s32[]{:S(2)}) async-start(s8[12582912]{0:T(1024)(128)(4,1)} %bitcast.95), calls=%async_computation.8 | async-start | bytes 8388608
  705.3 7.5 slice-start.2
  705.3 8.8 %slice-start.5 = ((s8[12582912]{0:T(1024)(128)(4,1)}), s8[4194304]{0:T(1024)(128)(4,1)S(1)}, s32[]{:S(2)}) async-start(s8[12582912]{0:T(1024)(128)(4,1)} %bitcast.95), calls=%async_computation.9 | async-start | bytes 8388608
where the time goes:
time: 783 us; the launch traced here: 776 us
  blocking collectives  381 us (49%)
  local copies, waits for them, and re-layouts  131 us (17%)
  other arithmetic  118 us (15%)
  waiting for transfers between devices  92.5 us (12%)
  matrix products  41.5 us (5%)
  starting transfers between devices  10.9 us (1%)
    all_to_all x1, blocking collectives, local(): lax.all_to_all(jnp.stack([potential, time_rate]), 'py', split_axis=1, con...  185 us
    all_to_all x1, blocking collectives, local(): lax.all_to_all(gradient, ('grp', 'px'), split_axis=3, concat_axis=2, tile...  143 us
    all_to_all x1, waiting for transfers between devices, local(): lax.all_to_all(spectral, 'py', split_axis=3, concat_axis=1, tiled=True)  92.5 us
    all_to_all x1, blocking collectives, local(): lax.all_to_all(payload, ('grp', 'px'), split_axis=2, concat_axis=3, tiled...  52.6 us
    unnamed x25, local copies, waits for them, and re-layouts  46.4 us
    all_to_all x2, local copies, waits for them, and re-layouts, local(): lax.all_to_all(gradient, ('grp', 'px'), split_axis=3, concat_axis=2, tile...  23.7 us
    sub x1, other arithmetic, local(): offset_field = auxiliary - multiplier / PENALTY  22.9 us
    another operation x1, local copies, waits for them, and re-layouts, local(): jnp.stack([space_values[1], jnp.roll(plane_potential, -1, axis=2) - plane...  21 us
  transfers between devices with their start and end apart: 3, of which 1 were waited for; matrix products, arithmetic and copies ran while one was open for 2% of the time, Pallas kernels for 0%

commit v1 on v0

--- a/solution.py
+++ b/solution.py
@@ -7,6 +7,18 @@
 NEWTON = 4
 PENALTY = 1.0
 PRECISE = lax.Precision.HIGHEST
+
+
+def in_blocks(shard, dim, peers):
+    shape = shard.shape
+    tiles = shard.reshape(*shape[:dim], peers, shape[dim] // peers, *shape[dim + 1 :])
+    return jnp.moveaxis(tiles, dim, 0)
+
+
+def laid_out(blocks, dim):
+    dims = list(blocks.shape[1:])
+    dims[dim] *= blocks.shape[0]
+    return jnp.moveaxis(blocks, 0, dim).reshape(dims)
 
 
 def passed_along(value, axis, steps):
@@ -102,7 +114,16 @@
     left_rim = from_behind(offset_along[:, :, rows_here - 1 :, :], ("grp", "px"), 1)
     beside = jnp.concatenate([left_rim, offset_along[:, :, : rows_here - 1, :]], axis=2)
     payload = (earlier - offset_time + beside - offset_along + source)[None]
-    pencil = lax.all_to_all(payload, ("grp", "px"), split_axis=2, concat_axis=3, tiled=True)
+    size, here = (lax.axis_size(("grp", "px")), lax.axis_index(("grp", "px")))
+    blocks = in_blocks(payload, 2, size)
+    gathered = [blocks[here]]
+    for step in range(1, size):
+        sent = blocks[here ^ step]
+        gathered.append(
+            lax.ppermute(sent, ("grp", "px"), [(i_2, i_2 ^ step) for i_2 in range(size)])
+        )
+    blocks = jnp.stack(gathered)[here ^ jnp.arange(size)]
+    pencil = laid_out(blocks, 3)
     row_count = pencil.shape[3]
     col_count = pencil.shape[4]
     hartley_rows = hartley_table(row_count)

time: 783 us -> 761 us (0.972)
  blocking collectives: 381 us -> 330 us
  waiting for transfers between devices: 92.5 us -> 131 us
  local copies, waits for them, and re-layouts: 131 us -> 116 us
  starting transfers between devices: 10.9 us -> 18.9 us
    all_to_all x1 -> x0, blocking collectives: 52.6 us -> none  [local(): lax.all_to_all(payload, ('grp', 'px'), split_axis=2, concat_axis=3, tiled...]
    ppermute x0 -> x7, waiting for transfers between devices: none -> 38 us  [local(): lax.ppermute(sent, ('grp', 'px'), [(i_2, i_2 ^ step) for i_2 in range(siz...]
    unnamed x25 -> x35, local copies, waits for them, and re-layouts: 46.4 us -> 20 us
    another operation x1 -> x0, other arithmetic: 20.6 us -> none  [project(): jnp.stack([jnp.where(feasible, time_part, time_part - (scaling - 1.0)), j...]
    add x0 -> x1, other arithmetic: none -> 14.4 us  [local(): multiplier_next = multiplier + PENALTY * (slab_gradient - auxiliary_next)]
    slice x0 -> x2, local copies, waits for them, and re-layouts: none -> 9.03 us  [the longest x1 6.39 us: local(): offset_time = jnp.where(level_index == levels - 1, 0.0, offset_field[0])]
    add x1, other arithmetic: 10.4 us -> 18.9 us  [local(): payload = (earlier - offset_time + beside - offset_along + source)[None]]
    all_to_all x2 -> x1, local copies, waits for them, and re-layouts: 23.7 us -> 16.6 us  [local(): lax.all_to_all(gradient, ('grp', 'px'), split_axis=3, concat_axis=2, tile...]
  transfers between devices with their start and end apart: 3 -> 10, of which waited for: 1 -> 4; matrix products, arithmetic and copies ran while one was open for 2% -> 5% of each run, Pallas kernels for 0% -> 0%
where the time goes in v1:
time: 761 us; the launch traced here: 754 us
  blocking collectives  330 us (43%)
  waiting for transfers between devices  131 us (17%)
  other arithmetic  116 us (15%)
  local copies, waits for them, and re-layouts  116 us (15%)
  matrix products  41.5 us (5%)
  starting transfers between devices  18.9 us (2%)
    all_to_all x1, blocking collectives, local(): lax.all_to_all(jnp.stack([potential, time_rate]), 'py', split_axis=1, con...  186 us
    all_to_all x1, blocking collectives, local(): lax.all_to_all(gradient, ('grp', 'px'), split_axis=3, concat_axis=2, tile...  144 us
    all_to_all x1, waiting for transfers between devices, local(): lax.all_to_all(spectral, 'py', split_axis=3, concat_axis=1, tiled=True)  93.2 us
    ppermute x7, waiting for transfers between devices, local(): lax.ppermute(sent, ('grp', 'px'), [(i_2, i_2 ^ step) for i_2 in range(siz...  38 us
    sub x1, other arithmetic, local(): offset_field = auxiliary - multiplier / PENALTY  22.9 us
    another operation x1, local copies, waits for them, and re-layouts, local(): jnp.stack([space_values[1], jnp.roll(plane_potential, -1, axis=2) - plane...  21 us
    unnamed x35, local copies, waits for them, and re-layouts  20 us
    add x1, other arithmetic, local(): payload = (earlier - offset_time + beside - offset_along + source)[None]  18.9 us
  transfers between devices with their start and end apart: 10, of which 4 were waited for; matrix products, arithmetic and copies ran while one was open for 5% of the time, Pallas kernels for 0%

profile of v1, /device:TPU:0, one launch (start us, length us, event | category | flops | bytes accessed | tf_op | source)
XLA Modules:
  0.0 754.2 jit_solution(4864248409760097866)
XLA Ops:
  0.6 22.9 %copy_subtract_fusion = f32[3,8,16,32,256]{4,1,2,3,0:T(8,128)S(1)} fusion(f32[3,8,16,32,256]{4,3,2,1,0:T(8,128)} %param.4, f32[3,8,16,32,256]{4,3,2,1,0:T(8,128)} %param.5), kind=kLoop, calls=%fused_computation.3 | loop fusion | flops 3145728 | bytes 37748736 | tf_op jit(solution)/shard_map/sub | solution.py:103
  27.5 5.8 collective-permute-start
  33.3 6.4 fusion.105
  45.6 3.9 copy.71
  49.5 4.3 copy.74
  56.4 6.5 copy.78
  64.5 18.9 %fusion.4 = f32[1,8,8,2,32,256]{5,4,3,1,2,0:T(8,128)S(1)} fusion(f32[1,7,8,2,32,256]{5,4,3,1,2,0:T(8,128)} %copy.71, f32[1,1,8,2,32,256]{5,4,3,1,2,0:T(8,128)S(1)} %bitcast.144, f32[1,8,8,2,31,256]{5,4,3,1,2,0:T(8,128)} %copy.74, f32[1,8,8,2,1,256]{5,4,3,1,2,0:T(1,128)S(1)} %copy.73, f32[1,8,8,2,32,255]{5,4,3,1,2,0:T(8,128)} %copy.78, ...), kind=kLoop, calls=%fused_computation.16 | loop fusion | flops 13631488 | bytes 30408720 | tf_op jit(solution)/shard_map/add | solution.py:116
  98.2 27.4 %collective-permute-done.3 = f32[1,8,2,32,256]{4,3,2,1,0:T(8,128)} collective-permute-done((f32[1,8,2,32,256]{4,3,2,1,0:T(8,128)S(1)}, f32[1,8,2,32,256]{4,3,2,1,0:T(8,128)}, u32[]{:S(2)}, u32[]{:S(2)}) %collective-permute-start.3) | collective-permute-done | bytes 524320 | tf_op jit(solution)/shard_map/ppermute | solution.py:123
  127.4 7.3 collective-permute-done.4
  136.4 3.4 collective-permute-done.6
  142.2 5.0 gather_fusion
  149.8 4.9 fusion.42
  154.6 4.6 fusion.31
  159.2 5.4 copy.81
  164.7 4.9 all-to-all-start
  170.4 93.2 %all-to-all-done = f32[1,8,2,256,256]{4,2,1,0,3:T(2,128)} async-done(((f32[1,8,2,256,256]{4,2,1,0,3:T(2,128)}), f32[1,8,2,256,256]{4,2,1,0,3:T(2,128)}, u32[]{:S(2)}, u32[]{:S(2)}) %all-to-all-start) | async-done | bytes 4194336 | tf_op jit(solution)/shard_map/all_to_all | solution.py:132
  263.6 6.0 fusion.6
  269.6 4.1 fusion.25
  273.7 4.1 fusion.28
  279.4 5.3 copy.84
  284.7 185.7 %all_to_all.51 = f32[2,32,2,64,256]{4,3,2,0,1:T(8,128)S(1)} all-to-all(f32[2,32,2,64,256]{4,3,2,0,1:T(8,128)S(1)} %copy.84), channel_id=1, replica_groups=mesh['grp'=2,'px'=4,'py'=4] {'py'}, dimensions={1} | all-to-all | bytes 16777216 | tf_op jit(solution)/shard_map/all_to_all | solution.py:143
  471.5 9.7 %fusion.45 = f32[256,2,8,2,256]{4,0,3,2,1:T(8,128)S(1)} fusion(f32[2,8,2,256,256]{4,3,2,1,0:T(8,128)S(1)} %bitcast.134), kind=kOutput, calls=%fused_computation.84 | convolution fusion | flops 6443499520 | bytes 16777216 | tf_op jit(solution)/shard_map/ctbxy,kx->ctbky/dot_general | solution.py:61
  481.2 8.1 %fusion = f32[2,8,2,256,256]{4,3,2,1,0:T(8,128)S(1)} fusion(f32[256,2,8,2,256]{4,0,3,2,1:T(8,128)S(1)} %fusion.45), kind=kOutput, calls=%fused_computation.6 | convolution fusion | flops 6443499520 | bytes 16777216 | tf_op jit(solution)/shard_map/ctbxy,ky->ctbxk/dot_general | solution.py:62
  499.8 10.0 %fusion.106 = (f32[1,8,2,256,256]{4,3,2,1,0:T(8,128)S(1)}, f32[1,8,2,256,256]{4,3,2,1,0:T(8,128)}, f32[1,8,2,256,256]{4,3,2,1,0:T(8,128)}) fusion(f32[2,8,2,256,256]{4,3,2,1,0:T(8,128)} %copy-done, f32[1,8,2,1,256]{4,3,2,1,0:T(1,128)S(1)} %slice_bitcast_fusion.3, f32[1,8,2,255,256]{4,3,2,1,0:T(8,128)} %slice_bitcast_fusion.1, ...), kind=kLoop, calls=%fused_computation.159 | loop fusion | flops 4194304 | bytes 29360128 | tf_op jit(solution)/shard_map/slice | solution.py:150
  509.8 9.7 %pad_maximum_fusion = f32[3,8,2,256,256]{4,3,2,1,0:T(8,128)} fusion(f32[1,8,2,256,256]{4,3,2,1,0:T(8,128)} %get-tuple-element.16, f32[1,8,2,256,256]{4,3,2,1,0:T(8,128)} %get-tuple-element.15, f32[1,8,2,256,256]{4,3,2,1,0:T(8,128)S(1)} %get-tuple-element.14), kind=kLoop, calls=%fused_computation.1 | loop fusion | flops 6291456 | bytes 25165824 | tf_op jit(solution)/shard_map/stack | solution.py:148
  519.5 21.0 %copy.89 = f32[3,8,2,256,256]{4,2,1,0,3:T(2,128)S(1)} copy(f32[3,8,2,256,256]{4,3,2,1,0:T(8,128)} %pad_maximum_fusion) | data formatting | bytes 25165824 | tf_op jit(solution)/shard_map/stack | solution.py:148
  540.5 143.9 %all_to_all.52 = f32[3,8,2,256,256]{4,2,1,0,3:T(2,128)} all-to-all(f32[3,8,2,256,256]{4,2,1,0,3:T(2,128)S(1)} %copy.89), channel_id=1, replica_groups=mesh['grp'=2,'px'=4,'py'=4] {'grp','px'}, dimensions={3} | all-to-all | bytes 25165824 | tf_op jit(solution)/shard_map/all_to_all | solution.py:155
  684.4 16.6 %copy.90 = f32[3,8,8,2,32,256]{5,4,3,2,1,0:T(8,128)} copy(f32[3,8,8,2,32,256]{5,3,1,0,4,2:T(2,128)} %bitcast.132) | data formatting | bytes 25165824 | tf_op jit(solution)/shard_map/all_to_all | solution.py:155
  701.0 14.9 %add.250 = f32[3,8,16,32,256]{4,3,2,1,0:T(8,128)} add(f32[3,8,16,32,256]{4,3,2,1,0:T(8,128)} %bitcast.128, f32[3,8,16,32,256]{4,3,2,1,0:T(8,128)} %param.4) | non-fusion elementwise | flops 3145728 | bytes 37748736 | tf_op jit(solution)/shard_map/add | solution.py:156
  715.9 14.8 %subtract_select_fusion = (f32[1,8,16,32,256]{4,3,2,1,0:T(8,128)}, f32[1,8,16,32,256]{4,3,2,1,0:T(8,128)S(1)}, pred[1,8,16,32,256]{4,3,2,1,0:T(8,128)(4,1)S(1)}) fusion(f32[3,8,16,32,256]{4,3,2,1,0:T(8,128)} %add.250), kind=kLoop, calls=%fused_computation.10 | loop fusion | flops 55574528 | bytes 22020096 | tf_op jit(solution)/shard_map/jit(_where)/select_n | solution.py:91
  730.7 7.6 %divide_select_fusion.1 = (f32[1,8,16,32,256]{4,3,2,1,0:T(8,128)}, f32[1,8,16,32,256]{4,3,2,1,0:T(8,128)}) fusion(pred[1,8,16,32,256]{4,3,2,1,0:T(8,128)(4,1)S(1)} %get-tuple-element.6, f32[1,8,16,32,256]{4,3,2,1,0:T(8,128)S(1)} %get-tuple-element.5, f32[3,8,16,32,256]{4,3,2,1,0:T(8,128)} %add.250), kind=kLoop, calls=%fused_computation.9 | loop fusion | flops 4194304 | bytes 22020096 | tf_op jit(solution)/shard_map/jit(_where)/select_n | solution.py:92
  739.5 14.4 %subtract_add_fusion = (f32[3,8,16,32,256]{4,3,2,1,0:T(8,128)}, f32[3,8,16,32,256]{4,3,2,1,0:T(8,128)}) fusion(f32[3,8,16,32,256]{4,3,2,1,0:T(8,128)S(1)} %bitcast.127, f32[3,8,16,32,256]{4,3,2,1,0:T(8,128)S(1)} %bitcast.131, f32[1,8,16,32,256]{4,3,2,1,0:T(8,128)} %get-tuple-element.8, f32[1,8,16,32,256]{4,3,2,1,0:T(8,128)} %get-tuple-element.7, ...), kind=kLoop, calls=%fused_computation.4 | loop fusion | flops 12582912 | bytes 62914560 | tf_op jit(solution)/shard_map/add | solution.py:158
  (87 shorter events, 52.4 us)
Async XLA Ops:
  24.1 2.0 copy-start.2
  27.5 35.6 %collective-permute-start = (f32[1,16,32,256]{3,0,1,2:T(1,128)}, f32[1,16,32,256]{3,0,1,2:T(1,128)}, u32[]{:S(2)}, u32[]{:S(2)}) collective-permute-start(f32[1,16,32,256]{3,0,1,2:T(1,128)} %slice.85), channel_id=1, source_target_pairs={{0,1},{1,2},{2,3},{4,5},{5,6},{6,7},{8,9},{9,10},{10,11},{12,13},{... | collective-permute-start | bytes 1572872 | tf_op jit(solution)/shard_map/ppermute | solution.py:27
  39.7 1.9 copy-start.5
  41.6 3.2 copy-start.7
  41.6 21.4 %collective-permute-start.1 = (f32[8,16,1,256]{3,0,1,2:T(8,128)S(1)}, f32[8,16,1,256]{3,0,1,2:T(8,128)S(1)}, u32[]{:S(2)}, u32[]{:S(2)}) collective-permute-start(f32[8,16,1,256]{3,0,1,2:T(8,128)S(1)} %slice.88), channel_id=1, source_target_pairs={{28,0},{0,4},{4,8},{8,12},{12,16},{16,20},{20,24},{24,28},{29,1},{... | collective-permute-start | bytes 393224 | tf_op jit(solution)/shard_map/ppermute | solution.py:33
  42.2 3.5 copy-start.3
  49.5 4.3 copy-start.1
  56.4 8.1 %copy-start.6 = (f32[16,32,256]{2,1,0:T(8,128)S(1)}, f32[16,32,256]{2,1,0:T(8,128)}, u32[]{:S(2)}) copy-start(f32[16,32,256]{2,1,0:T(8,128)} %param.7) | copy-start | bytes 1572868
  83.4 2.0 copy-start.4
  86.6 8.2 %collective-permute-start.2 = (f32[1,8,2,32,256]{4,3,2,1,0:T(8,128)}, f32[1,8,2,32,256]{4,3,2,1,0:T(8,128)}, u32[]{:S(2)}, u32[]{:S(2)}) collective-permute-start(f32[1,8,2,32,256]{4,3,2,1,0:T(8,128)} %get-tuple-element.23), channel_id=1, source_target_pairs={{0,4},{4,0},{8,12},{12,8},{16,20},{20,16},{24,28},{28,24},{1,5},{5... | collective-permute-start | bytes 1572872 | tf_op jit(solution)/shard_map/ppermute | solution.py:123
  88.1 37.4 %collective-permute-start.3 = (f32[1,8,2,32,256]{4,3,2,1,0:T(8,128)S(1)}, f32[1,8,2,32,256]{4,3,2,1,0:T(8,128)}, u32[]{:S(2)}, u32[]{:S(2)}) collective-permute-start(f32[1,8,2,32,256]{4,3,2,1,0:T(8,128)S(1)} %get-tuple-element.22), channel_id=1, source_target_pairs={{0,8},{4,12},{8,0},{12,4},{16,24},{20,28},{24,16},{28,20},{1,9},{5... | collective-permute-start | bytes 1572872 | tf_op jit(solution)/shard_map/ppermute | solution.py:123
  89.6 45.1 %collective-permute-start.4 = (f32[1,8,2,32,256]{4,3,2,1,0:T(8,128)S(1)}, f32[1,8,2,32,256]{4,3,2,1,0:T(8,128)S(1)}, u32[]{:S(2)}, u32[]{:S(2)}) collective-permute-start(f32[1,8,2,32,256]{4,3,2,1,0:T(8,128)S(1)} %get-tuple-element.21), channel_id=1, source_target_pairs={{0,12},{4,8},{8,4},{12,0},{16,28},{20,24},{24,20},{28,16},{1,13},{... | collective-permute-start | bytes 1572872 | tf_op jit(solution)/shard_map/ppermute | solution.py:123
  91.6 49.9 %collective-permute-start.8 = (f32[1,8,2,32,256]{4,3,2,1,0:T(8,128)S(1)}, f32[1,8,2,32,256]{4,3,2,1,0:T(8,128)S(1)}, u32[]{:S(2)}, u32[]{:S(2)}) collective-permute-start(f32[1,8,2,32,256]{4,3,2,1,0:T(8,128)S(1)} %get-tuple-element.17), channel_id=1, source_target_pairs={{0,28},{4,24},{8,20},{12,16},{16,12},{20,8},{24,4},{28,0},{1,29},{... | collective-permute-start | bytes 1572872 | tf_op jit(solution)/shard_map/ppermute | solution.py:123
  93.3 47.3 %collective-permute-start.7 = (f32[1,8,2,32,256]{4,3,2,1,0:T(8,128)S(1)}, f32[1,8,2,32,256]{4,3,2,1,0:T(8,128)S(1)}, u32[]{:S(2)}, u32[]{:S(2)}) collective-permute-start(f32[1,8,2,32,256]{4,3,2,1,0:T(8,128)S(1)} %get-tuple-element.18), channel_id=1, source_target_pairs={{0,24},{4,28},{8,16},{12,20},{16,8},{20,12},{24,0},{28,4},{1,25},{... | collective-permute-start | bytes 1572872 | tf_op jit(solution)/shard_map/ppermute | solution.py:123
  94.8 40.8 %collective-permute-start.5 = (f32[1,8,2,32,256]{4,3,2,1,0:T(8,128)S(1)}, f32[1,8,2,32,256]{4,3,2,1,0:T(8,128)S(1)}, u32[]{:S(2)}, u32[]{:S(2)}) collective-permute-start(f32[1,8,2,32,256]{4,3,2,1,0:T(8,128)S(1)} %get-tuple-element.20), channel_id=1, source_target_pairs={{0,16},{4,20},{8,24},{12,28},{16,0},{20,4},{24,8},{28,12},{1,17},{... | collective-permute-start | bytes 1572872 | tf_op jit(solution)/shard_map/ppermute | solution.py:123
  125.5 14.2 %collective-permute-start.6 = (f32[1,8,2,32,256]{4,3,2,1,0:T(8,128)S(1)}, f32[1,8,2,32,256]{4,3,2,1,0:T(8,128)S(1)}, u32[]{:S(2)}, u32[]{:S(2)}) collective-permute-start(f32[1,8,2,32,256]{4,3,2,1,0:T(8,128)S(1)} %get-tuple-element.19), channel_id=1, source_target_pairs={{0,20},{4,16},{8,28},{12,24},{16,4},{20,0},{24,12},{28,8},{1,21},{... | collective-permute-start | bytes 1572872 | tf_op jit(solution)/shard_map/ppermute | solution.py:123
  164.7 98.9 %all-to-all-start = ((f32[1,8,2,256,256]{4,2,1,0,3:T(2,128)}), f32[1,8,2,256,256]{4,2,1,0,3:T(2,128)}, u32[]{:S(2)}, u32[]{:S(2)}) async-start(f32[1,8,2,256,256]{4,2,1,0,3:T(2,128)} %copy.81), calls=%async_computation | async-start | bytes 8388608 | tf_op jit(solution)/shard_map/all_to_all | solution.py:132
  489.4 3.4 copy-start
  715.9 22.4 %slice-start = ((s8[12582912]{0:T(1024)(128)(4,1)}), s8[4194304]{0:T(1024)(128)(4,1)S(1)}, s32[]{:S(2)}) async-start(s8[12582912]{0:T(1024)(128)(4,1)} %bitcast.126), calls=%async_computation.3 | async-start | bytes 8388608
  715.9 22.4 %slice-start.1 = ((s8[12582912]{0:T(1024)(128)(4,1)}), s8[4194304]{0:T(1024)(128)(4,1)S(1)}, s32[]{:S(2)}) async-start(s8[12582912]{0:T(1024)(128)(4,1)} %bitcast.126), calls=%async_computation.4 | async-start | bytes 8388608
  715.9 22.4 %slice-start.3 = ((s8[12582912]{0:T(1024)(128)(4,1)}), s8[4194304]{0:T(1024)(128)(4,1)S(1)}, s32[]{:S(2)}) async-start(s8[12582912]{0:T(1024)(128)(4,1)} %bitcast.129), calls=%async_computation.6 | async-start | bytes 8388608
  715.9 22.4 %slice-start.4 = ((s8[12582912]{0:T(1024)(128)(4,1)}), s8[4194304]{0:T(1024)(128)(4,1)S(1)}, s32[]{:S(2)}) async-start(s8[12582912]{0:T(1024)(128)(4,1)} %bitcast.129), calls=%async_computation.7 | async-start | bytes 8388608
  730.7 7.6 %slice-start.2 = ((s8[12582912]{0:T(1024)(128)(4,1)}), s8[4194304]{0:T(1024)(128)(4,1)S(1)}, s32[]{:S(2)}) async-start(s8[12582912]{0:T(1024)(128)(4,1)} %bitcast.126), calls=%async_computation.5 | async-start | bytes 8388608
  730.7 8.8 %slice-start.5 = ((s8[12582912]{0:T(1024)(128)(4,1)}), s8[4194304]{0:T(1024)(128)(4,1)S(1)}, s32[]{:S(2)}) async-start(s8[12582912]{0:T(1024)(128)(4,1)} %bitcast.129), calls=%async_computation.8 | async-start | bytes 8388608
